TPU v7x, 32 devices: a whole 2x2x4 slice. The times are simulated.
32 devices in a mesh: replica: 8 (over y, x, core), tensor: 4 (over z).
Axes of the slice: x: 2, y: 2, z: 4, core: 2. Of those that a mesh axis runs over, the one named last changes fastest.
Arguments:
- queries: bfloat16 [8, 512, 2560], P('replica', None, 'tensor'), may hold values from -160 to 160
- key_rows: bfloat16 [8, 512, 2560], P('replica', None, 'tensor'), may hold values from -4 to 4
- value_rows: bfloat16 [8, 512, 2560], P('replica', None, 'tensor'), may hold values from -6 to 6
- out_grads: bfloat16 [8, 512, 1024], P('replica', 'tensor'), may hold values from -6 to 6
- inner_weights: bfloat16 [8, 20, 128, 1024], P('replica', 'tensor'), may hold values from -0.15625 to 0.15625
- adam_first: bfloat16 [8, 20, 128, 1024], P('replica', 'tensor'), may hold values from -12 to 12
- adam_second: bfloat16 [8, 20, 128, 1024], P('replica', 'tensor'), may hold values from 1 to 16
- anchor: bfloat16 [20, 128, 1024], P('tensor'), may hold values from -0.125 to 0.125
- momentum: float32 [20, 128, 1024], P('tensor', 'replica'), may hold values from -0.06 to 0.06
Outputs:
- query_grads: bfloat16 [8, 512, 2560], P('replica', None, 'tensor')
- key_grads: bfloat16 [8, 512, 2560], P('replica', None, 'tensor')
- value_grads: bfloat16 [8, 512, 2560], P('replica', None, 'tensor')
- new_first: bfloat16 [8, 20, 128, 1024], P('replica', 'tensor')
- new_second: bfloat16 [8, 20, 128, 1024], P('replica', 'tensor')
- new_anchor: bfloat16 [20, 128, 1024], P('tensor')
- new_momentum: float32 [20, 128, 1024], P('tensor', 'replica')
All inputs are finite; a program needn't handle non-finite values.
Results may differ from a plain program's by a relative error of at most 0.028.
Values may be sent and summed in bfloat16 or wider, within the bound.
A program may use at most 64 MiB of HBM per device.

v0:
```python
import math
import jax
import jax.numpy as jnp
from jax import lax
from jax.sharding import PartitionSpec as P

DH = 128
beta_first = 0.9
beta_second = 0.95
correct_first = 0.9999734386011124
correct_second = 0.994079470779666
inner_rate = 0.01
decay_rate = 0.1
epsilon = 1e-08
outer_rate = 0.7
outer_beta = 0.9


def local(
    queries,
    key_rows,
    value_rows,
    out_grads,
    inner_weights,
    adam_first,
    adam_second,
    anchor,
    momentum,
):
    length = queries.shape[1]
    inner_width = queries.shape[2]
    head_count = inner_width // DH
    model_width = out_grads.shape[2]
    score_scale = 1.0 / math.sqrt(DH)
    query_heads = queries[0].reshape(length, head_count, DH)
    key_heads = key_rows[0].reshape(length, head_count, DH)
    value_heads = value_rows[0].reshape(length, head_count, DH)
    scores = (
        jnp.einsum("qhc,khc->hqk", query_heads, key_heads, preferred_element_type=jnp.float32)
        * score_scale
    )
    probs = jax.nn.softmax(scores, axis=-1)
    probs_low = probs.astype(jnp.bfloat16)
    attention = jnp.einsum(
        "hqk,khc->qhc", probs_low, value_heads, preferred_element_type=jnp.float32
    ).astype(jnp.bfloat16)
    attention_rows = attention.reshape(length, inner_width)
    proj_rows = inner_weights[0].reshape(inner_width, model_width)
    block_rows = lax.all_gather(out_grads[0], "tensor", axis=0, tiled=True)
    product_rows = lax.dot_general(
        block_rows, proj_rows, (((1,), (1,)), ((), ())), preferred_element_type=jnp.float32
    ).astype(jnp.bfloat16)
    grad_rows = product_rows
    gradient = lax.dot_general(
        attention_rows, block_rows, (((0,), (0,)), ((), ())), preferred_element_type=jnp.float32
    )
    grad_rows, gradient = (grad_rows, gradient)
    grad_attn = grad_rows.reshape(length, head_count, DH)
    value_grads = jnp.einsum(
        "hqk,qhc->khc", probs_low, grad_attn, preferred_element_type=jnp.float32
    ).astype(jnp.bfloat16)
    grad_probs = jnp.einsum(
        "qhc,khc->hqk", grad_attn, value_heads, preferred_element_type=jnp.float32
    )
    row_dot = jnp.einsum("qhc,qhc->hq", grad_attn, attention, preferred_element_type=jnp.float32)
    grad_scores = (probs * (grad_probs - row_dot[:, :, None])).astype(jnp.bfloat16)
    query_grads = (
        jnp.einsum("hqk,khc->qhc", grad_scores, key_heads, preferred_element_type=jnp.float32)
        * score_scale
    ).astype(jnp.bfloat16)
    key_grads = (
        jnp.einsum("hqk,qhc->khc", grad_scores, query_heads, preferred_element_type=jnp.float32)
        * score_scale
    ).astype(jnp.bfloat16)
    grad_proj = gradient.reshape(head_count, DH, model_width)
    first_moment = beta_first * adam_first[0].astype(jnp.float32) + (1.0 - beta_first) * grad_proj
    second_moment = (
        beta_second * adam_second[0].astype(jnp.float32)
        + (1.0 - beta_second) * grad_proj * grad_proj
    )
    previous = inner_weights[0].astype(jnp.float32)
    stepped = previous - inner_rate * (
        first_moment / correct_first / (jnp.sqrt(second_moment / correct_second) + epsilon)
        + decay_rate * previous
    )
    anchor_wide = anchor.astype(jnp.float32)
    delta_terms = (anchor_wide - stepped).astype(jnp.bfloat16).astype(jnp.float32)
    workers = lax.axis_size("replica")
    slab = momentum.shape[1]
    portion = lax.psum_scatter(
        delta_terms.astype(jnp.bfloat16), "replica", scatter_dimension=1, tiled=True
    ).astype(jnp.float32)
    average = portion / workers
    new_momentum = outer_beta * momentum + average
    anchor_part = lax.dynamic_slice_in_dim(anchor_wide, lax.axis_index("replica") * slab, slab, 1)
    updated = (anchor_part - outer_rate * (average + outer_beta * new_momentum)).astype(
        jnp.bfloat16
    )
    new_anchor = lax.all_gather(updated, "replica", axis=1, tiled=True)
    return (
        query_grads.reshape(length, inner_width)[None],
        key_grads.reshape(length, inner_width)[None],
        value_grads.reshape(length, inner_width)[None],
        first_moment.astype(jnp.bfloat16)[None],
        second_moment.astype(jnp.bfloat16)[None],
        new_anchor,
        new_momentum,
    )


def solution(mesh):
    in_specs = (
        P("replica", None, "tensor"),
        P("replica", None, "tensor"),
        P("replica", None, "tensor"),
        P("replica", "tensor", None),
        P("replica", "tensor", None, None),
        P("replica", "tensor", None, None),
        P("replica", "tensor", None, None),
        P("tensor", None, None),
        P("tensor", "replica", None),
    )
    out_specs = (
        P("replica", None, "tensor"),
        P("replica", None, "tensor"),
        P("replica", None, "tensor"),
        P("replica", "tensor", None, None),
        P("replica", "tensor", None, None),
        P("tensor", None, None),
        P("tensor", "replica", None),
    )
    return jax.shard_map(local, mesh=mesh, in_specs=in_specs, out_specs=out_specs, check_vma=False)
```

profile of v0, /device:TPU:0, one launch (start us, length us, event | category | flops | bytes accessed | tf_op | source)
XLA Modules:
  0.0 125.8 jit_solution(16689872000383346448)
XLA Ops:
  7.2 0.7 all-gather.6.cloned.1.call-update
  8.0 1.3 %copy.32 = bf16[1,512,640]{1,2,0:T(8,128)(2,1)S(1)} copy(bf16[1,512,640]{2,1,0:T(8,128)(2,1)} %param.9) | data formatting | bytes 1310720 | tf_op args[0]
  9.3 1.6 %copy.33 = bf16[1,512,640]{1,2,0:T(8,128)(2,1)S(1)} copy(bf16[1,512,640]{2,1,0:T(8,128)(2,1)} %param.10) | data formatting | bytes 1310720 | tf_op args[1]
  10.9 1.1 copy.37
  12.0 4.1 %fusion.25 = (f32[5,512]{1,0:T(8,128)S(1)}, f32[5,512,512]{1,2,0:T(8,128)}) fusion(bf16[512,5,128]{0,2,1:T(8,128)(2,1)S(1)} %bitcast.86, bf16[512,5,128]{0,2,1:T(8,128)(2,1)S(1)} %bitcast.82), kind=kOutput, calls=%fused_computation.39 | convolution fusion | flops 339476992 | bytes 6563840 | tf_op jit(solution)/shard_map/sub | solution.py:42
  16.1 3.2 %fusion.10 = bf16[5,512,512]{1,2,0:T(8,128)(2,1)S(1)} fusion(f32[5,512,512]{1,2,0:T(8,128)} %get-tuple-element.27, f32[5,512]{1,0:T(8,128)S(1)} %get-tuple-element.26), kind=kLoop, calls=%fused_computation.16 | loop fusion | flops 2621440 | bytes 7874560 | tf_op jit(solution)/shard_map/convert_element_type | solution.py:43
  19.3 20.9 %all-gather.6.cloned.1.call-done = bf16[1,512,1024]{2,1,0:T(8,128)(2,1)} async-done(((bf16[1,128,1024]{2,1,0:T(8,128)(2,1)}), bf16[1,512,1024]{2,1,0:T(8,128)(2,1)}) %all-gather.6.cloned.1.call-update) | async-done | bytes 1048592 | tf_op jit(solution)/shard_map/all_gather | solution.py:49
  40.3 3.5 %convolution_convert_fusion = bf16[512,640]{1,0:T(8,128)(2,1)} fusion(bf16[640,1024]{1,0:T(8,128)(2,1)} %bitcast.89, bf16[1,512,1024]{2,1,0:T(8,128)(2,1)} %all-gather.6.cloned.1.call-done), kind=kOutput, calls=%fused_computation.22 | convolution fusion | flops 671416320 | bytes 3014656 | tf_op jit(solution)/shard_map/dot_general | solution.py:50
  43.8 1.3 %copy.36 = bf16[512,640]{0,1:T(8,128)(2,1)S(1)} copy(bf16[512,640]{1,0:T(8,128)(2,1)} %convolution_convert_fusion) | data formatting | bytes 1310720 | tf_op jit(solution)/shard_map/convert_element_type | solution.py:52
  45.2 1.8 %fusion.17 = (f32[5,512]{1,0:T(8,128)S(1)}, bf16[5,512,128]{1,2,0:T(8,128)(2,1)S(1)}) fusion(bf16[5,512,128]{1,2,0:T(8,128)(2,1)S(1)} %bitcast.77, bf16[512,5,128]{0,2,1:T(8,128)(2,1)} %bitcast.80, bf16[5,512,512]{1,2,0:T(8,128)(2,1)S(1)} %fusion.10), kind=kOutput, calls=%fused_computation.29 | convolution fusion | flops 337180160 | bytes 4597760 | tf_op jit(solution)/shard_map/hqk,khc->qhc/dot_general | solution.py:44
  47.4 5.9 %fusion.7 = (bf16[5,128,1024]{2,1,0:T(8,128)(2,1)}, bf16[1,5,128,1024]{3,2,1,0:T(8,128)(2,1)}, bf16[1,5,128,1024]{3,2,1,0:T(8,128)(2,1)}) fusion(bf16[1,5,128,1024]{3,2,1,0:T(8,128)(2,1)S(1)} %copy-done.7, bf16[1,5,128,1024]{3,2,1,0:T(8,128)(2,1)} %param.15, bf16[1,5,128,1024]{3,2,1,0:T(8,128)(2,1)S(1)} %copy-done.6, ...), kind=kOutput, calls=%fused_computation.11 | convolution fusion | flops 686161920 | bytes 10878976 | tf_op jit(solution)/shard_map/dot_general | solution.py:54
  53.4 3.1 %convert_element_type.82 = f32[5,128,1024]{2,1,0:T(8,128)} convert(bf16[5,128,1024]{2,1,0:T(8,128)(2,1)} %param.16) | non-fusion elementwise | flops 655360 | bytes 3932160 | tf_op jit(solution)/shard_map/convert_element_type | solution.py:86
  56.5 33.6 %reduce-scatter.2.cloned.1.call-done = bf16[5,16,1024]{2,1,0:T(8,128)(2,1)} async-done(((bf16[5,128,1024]{2,1,0:T(8,128)(2,1)}), bf16[5,16,1024]{2,1,0:T(8,128)(2,1)}) %reduce-scatter.2.cloned.1.call-update) | async-done | bytes 163856 | tf_op jit(solution)/shard_map/reduce_scatter | solution.py:90
  90.1 2.0 %subtract_convert_fusion = (bf16[5,16,1024]{2,1,0:T(8,128)(2,1)}, f32[5,16,1024]{2,1,0:T(8,128)}) fusion(bf16[5,16,1024]{2,1,0:T(8,128)(2,1)} %reduce-scatter.2.cloned.1.call-done, f32[5,128,1024]{2,1,0:T(8,128)} %convert_element_type.82, s32[]{:T(128)S(6)} %select_n.3, f32[5,16,1024]{2,1,0:T(8,128)} %param.17), kind=kLoop, calls=%fused_computation.35 | loop fusion | flops 737280 | bytes 1310724 | tf_op jit(solution)/shard_map/convert_element_type | solution.py:96
  92.1 3.7 %multiply_convert_fusion = bf16[5,512,512]{1,2,0:T(8,128)(2,1)S(1)} fusion(f32[5,512]{1,0:T(8,128)S(1)} %get-tuple-element.28, bf16[512,5,128]{0,2,1:T(8,128)(2,1)S(1)} %bitcast.78, bf16[512,5,128]{0,2,1:T(8,128)(2,1)} %bitcast.81, f32[5,512,512]{1,2,0:T(8,128)} %get-tuple-element.27, f32[5,512]{1,0:T(8,128)S(1)} %get-tuple-element.26), kind=kOutput, calls=%fused_computation.1 | convolution fusion | flops 340787200 | bytes 9195520 | tf_op jit(solution)/shard_map/qhc,khc->hqk/dot_general | solution.py:62
  95.8 1.5 %copy-done = bf16[5,512,512]{1,2,0:T(8,128)(2,1)} copy-done((bf16[5,512,512]{1,2,0:T(8,128)(2,1)}, bf16[5,512,512]{1,2,0:T(8,128)(2,1)S(1)}, u32[]{:S(2)}) %copy-start) | copy-done | bytes 2621464
  97.3 1.8 %fusion.12 = bf16[5,512,128]{1,2,0:T(8,128)(2,1)} fusion(bf16[5,512,512]{1,2,0:T(8,128)(2,1)S(1)} %multiply_convert_fusion, bf16[512,5,128]{0,2,1:T(8,128)(2,1)S(1)} %bitcast.87), kind=kOutput, calls=%fused_computation.20 | convolution fusion | flops 336199680 | bytes 3932160 | tf_op jit(solution)/shard_map/hqk,qhc->khc/dot_general | solution.py:72
  99.1 2.2 %copy.46 = bf16[1,512,640]{2,1,0:T(8,128)(2,1)} copy(bf16[1,512,640]{1,2,0:T(8,128)(2,1)} %bitcast.88) | data formatting | bytes 1310720
  101.3 3.3 %fusion.13 = bf16[5,512,128]{1,2,0:T(8,128)(2,1)} fusion(bf16[512,5,128]{0,2,1:T(8,128)(2,1)} %bitcast.83, bf16[5,512,512]{1,2,0:T(8,128)(2,1)} %copy-done), kind=kOutput, calls=%fused_computation.21 | convolution fusion | flops 336199680 | bytes 3932160 | tf_op jit(solution)/shard_map/hqk,khc->qhc/dot_general | solution.py:68
  104.6 2.2 %copy.45 = bf16[1,512,640]{2,1,0:T(8,128)(2,1)} copy(bf16[1,512,640]{1,2,0:T(8,128)(2,1)} %bitcast.84) | data formatting | bytes 1310720
  106.8 1.8 %convolution_convert_fusion.2 = bf16[5,128,512]{2,1,0:T(8,128)(2,1)} fusion(bf16[512,5,128]{0,2,1:T(8,128)(2,1)S(1)} %bitcast.79, bf16[5,512,512]{1,2,0:T(8,128)(2,1)S(1)} %fusion.10), kind=kOutput, calls=%fused_computation.24 | convolution fusion | flops 335872000 | bytes 3932160 | tf_op jit(solution)/shard_map/hqk,qhc->khc/dot_general | solution.py:59
  108.6 2.2 %copy.47 = bf16[1,512,640]{2,1,0:T(8,128)(2,1)} copy(bf16[1,512,640]{1,2,0:T(8,128)(2,1)} %bitcast.85) | data formatting | bytes 1310720
  110.7 6.0 %all-gather.4.cloned.1.call-done = bf16[5,128,1024]{2,1,0:T(8,128)(2,1)} async-done(((bf16[5,16,1024]{2,1,0:T(8,128)(2,1)}), bf16[5,128,1024]{2,1,0:T(8,128)(2,1)}) %all-gather.4.cloned.1.call-update) | async-done | bytes 1310736 | tf_op jit(solution)/shard_map/all_gather | solution.py:99
  116.7 2.5 %copy.67 = bf16[5,128,1024]{2,1,0:T(8,128)(2,1)} copy(bf16[5,128,1024]{2,1,0:T(8,128)(2,1)} %all-gather.4.cloned.1.call-done) | data formatting | bytes 2621440
  (20 shorter events, 0.7 us)
Async XLA Ops:
  7.2 3.7 %copy-start.3 = (bf16[1,512,640]{2,1,0:T(8,128)(2,1)S(1)}, bf16[1,512,640]{2,1,0:T(8,128)(2,1)}, u32[]{:S(2)}) copy-start(bf16[1,512,640]{2,1,0:T(8,128)(2,1)} %param.11) | copy-start | bytes 1966084
  7.2 33.1 %all-gather.6.cloned.1.call-start = ((), (), s32[]{:S(2)}) async-start(), calls=%async_computation.3 | async-start | bytes 1310720 | tf_op jit(solution)/shard_map/all_gather | solution.py:49
  7.9 82.2 %reduce-scatter.2.cloned.1.call-start = ((), (), s32[]{:S(2)}) async-start(), calls=%async_computation.1 | async-start | bytes 1474560 | tf_op jit(solution)/shard_map/reduce_scatter | solution.py:90
  9.3 6.8 %copy-start.4 = (bf16[1,512,640]{1,2,0:T(8,128)(2,1)}, bf16[1,512,640]{1,2,0:T(8,128)(2,1)S(1)}, u32[]{:S(2)}) copy-start(bf16[1,512,640]{1,2,0:T(8,128)(2,1)S(1)} %copy.32) | copy-start | bytes 1966084
  10.9 5.2 %copy-start.1 = (bf16[1,512,640]{1,2,0:T(8,128)(2,1)}, bf16[1,512,640]{1,2,0:T(8,128)(2,1)S(1)}, u32[]{:S(2)}) copy-start(bf16[1,512,640]{1,2,0:T(8,128)(2,1)S(1)} %copy.33) | copy-start | bytes 1966084
  45.1 1.8 %copy-start.2 = (bf16[5,128,1024]{2,1,0:T(8,128)(2,1)S(1)}, bf16[5,128,1024]{2,1,0:T(8,128)(2,1)}, u32[]{:S(2)}) copy-start(bf16[5,128,1024]{2,1,0:T(8,128)(2,1)} %param.16) | copy-start | bytes 3932164
  45.1 1.9 %copy-start.6 = (bf16[1,5,128,1024]{3,2,1,0:T(8,128)(2,1)S(1)}, bf16[1,5,128,1024]{3,2,1,0:T(8,128)(2,1)}, u32[]{:S(2)}) copy-start(bf16[1,5,128,1024]{3,2,1,0:T(8,128)(2,1)} %param.13) | copy-start | bytes 3932164
  45.1 2.3 %copy-start.7 = (bf16[1,5,128,1024]{3,2,1,0:T(8,128)(2,1)S(1)}, bf16[1,5,128,1024]{3,2,1,0:T(8,128)(2,1)}, u32[]{:S(2)}) copy-start(bf16[1,5,128,1024]{3,2,1,0:T(8,128)(2,1)} %param.14) | copy-start | bytes 3932164
  53.3 63.4 %all-gather.4.cloned.1.call-start = ((), (), s32[]{:S(2)}) async-start(), calls=%async_computation.2 | async-start | bytes 1474560 | tf_op jit(solution)/shard_map/all_gather | solution.py:99
  92.1 5.2 %copy-start.5 = (bf16[1,512,640]{1,2,0:T(8,128)(2,1)S(1)}, bf16[1,512,640]{1,2,0:T(8,128)(2,1)}, u32[]{:S(2)}) copy-start(bf16[1,512,640]{1,2,0:T(8,128)(2,1)} %copy-done.4) | copy-start | bytes 1966084
  95.8 1.5 %copy-start = (bf16[5,512,512]{1,2,0:T(8,128)(2,1)}, bf16[5,512,512]{1,2,0:T(8,128)(2,1)S(1)}, u32[]{:S(2)}) copy-start(bf16[5,512,512]{1,2,0:T(8,128)(2,1)S(1)} %multiply_convert_fusion) | copy-start | bytes 7864324
Sparse Core Ops, SparseCore 0:
  9.6 30.6 all-gather.5
  53.5 36.5 reduce-scatter.1
  92.2 24.4 all-gather.3
where the time goes:
time: 126 us
  waiting for transfers between devices  61.2 us (49%)
  matrix products  25.9 us (21%)
  local copies, waits for them, and re-layouts  16.4 us (13%)
  between operations  13.9 us (11%)
  other arithmetic  8.35 us (7%)
    reduce_scatter x1, waiting for transfers between devices, local(): lax.psum_scatter(delta_terms.astype(jnp.bfloat16), 'replica', scatter_dim...  33.6 us
    all_gather x1, waiting for transfers between devices, local(): block_rows = lax.all_gather(out_grads[0], 'tensor', axis=0, tiled=True)  20.9 us
    unnamed x23, local copies, waits for them, and re-layouts  15 us
    all_gather x1, waiting for transfers between devices, local(): new_anchor = lax.all_gather(updated, 'replica', axis=1, tiled=True)  5.99 us
    dot_general x1, matrix products, local(): lax.dot_general(attention_rows, block_rows, (((0,), (0,)), ((), ())), pre...  5.87 us
    sub x1, matrix products, local(): probs = jax.nn.softmax(scores, axis=-1)  4.12 us
    dot_general x1, matrix products, local(): jnp.einsum('qhc,khc->hqk', grad_attn, value_heads, preferred_element_type...  3.67 us
    dot_general x1, matrix products, local(): lax.dot_general(block_rows, proj_rows, (((1,), (1,)), ((), ())), preferre...  3.49 us
  transfers between devices with their start and end apart: 3, of which 3 were waited for; matrix products, arithmetic and copies ran while one was open for 25% of the time, Pallas kernels for 0%

commit v1 on v0

--- a/solution.py
+++ b/solution.py
@@ -46,7 +46,14 @@
     ).astype(jnp.bfloat16)
     attention_rows = attention.reshape(length, inner_width)
     proj_rows = inner_weights[0].reshape(inner_width, model_width)
-    block_rows = lax.all_gather(out_grads[0], "tensor", axis=0, tiled=True)
+    ring = [out_grads[0]]
+    for hop in range(3):
+        ring.append(lax.ppermute(ring[-1], "tensor", [(dev, (dev + 1) % 4) for dev in range(4)]))
+    block_rows = jnp.roll(
+        jnp.concatenate(ring[::-1], axis=0),
+        (lax.axis_index("tensor") + 1) * ring[0].shape[0],
+        axis=0,
+    )
     product_rows = lax.dot_general(
         block_rows, proj_rows, (((1,), (1,)), ((), ())), preferred_element_type=jnp.float32
     ).astype(jnp.bfloat16)

time: 126 us -> 115 us (0.913)
  waiting for transfers between devices: 61.2 us -> 46.1 us
  starting transfers between devices: 0.12 us -> 3.34 us
  matrix products: 25.9 us -> 23.3 us
  local copies, waits for them, and re-layouts: 16.4 us -> 18.2 us
    all_gather x1 -> x0, waiting for transfers between devices: 20.9 us -> none  [local(): block_rows = lax.all_gather(out_grads[0], 'tensor', axis=0, tiled=True)]
    ppermute x0 -> x3, waiting for transfers between devices: none -> 14.2 us  [local(): lax.ppermute(ring[-1], 'tensor', [(dev, (dev + 1) % 4) for dev in range(4)])]
    all_gather x1, waiting for transfers between devices: 5.99 us -> 0.01 us  [local(): new_anchor = lax.all_gather(updated, 'replica', axis=1, tiled=True)]
    ppermute x0 -> x3, starting transfers between devices: none -> 3.26 us  [local(): lax.ppermute(ring[-1], 'tensor', [(dev, (dev + 1) % 4) for dev in range(4)])]
    dot_general x1, matrix products: 3.32 us -> 1.39 us  [local(): jnp.einsum('hqk,khc->qhc', grad_scores, key_heads, preferred_element_type...]
    dot_general x1, matrix products: 1.81 us -> 3.69 us  [local(): jnp.einsum('hqk,qhc->khc', grad_scores, query_heads, preferred_element_ty...]
    unnamed x23 -> x40, local copies, waits for them, and re-layouts: 15 us -> 16.8 us
    reduce_scatter x1, waiting for transfers between devices: 33.6 us -> 31.9 us  [local(): lax.psum_scatter(delta_terms.astype(jnp.bfloat16), 'replica', scatter_dim...]
  transfers between devices with their start and end apart: 3 -> 5, of which waited for: 3 -> 4; matrix products, arithmetic and copies ran while one was open for 25% -> 34% of each run, Pallas kernels for 0% -> 0%
where the time goes in v1:
time: 115 us
  waiting for transfers between devices  46.1 us (40%)
  matrix products  23.3 us (20%)
  local copies, waits for them, and re-layouts  18.2 us (16%)
  between operations  14.3 us (12%)
  other arithmetic  9.57 us (8%)
  starting transfers between devices  3.34 us (3%)
    reduce_scatter x1, waiting for transfers between devices, local(): lax.psum_scatter(delta_terms.astype(jnp.bfloat16), 'replica', scatter_dim...  31.9 us
    unnamed x40, local copies, waits for them, and re-layouts  16.8 us
    ppermute x3, waiting for transfers between devices, local(): lax.ppermute(ring[-1], 'tensor', [(dev, (dev + 1) % 4) for dev in range(4)])  14.2 us
    dot_general x1, matrix products, local(): lax.dot_general(attention_rows, block_rows, (((0,), (0,)), ((), ())), pre...  4.46 us
    sub x1, matrix products, local(): probs = jax.nn.softmax(scores, axis=-1)  4.13 us
    dot_general x1, matrix products, local(): jnp.einsum('qhc,khc->hqk', grad_attn, value_heads, preferred_element_type...  3.79 us
    dot_general x1, matrix products, local(): jnp.einsum('hqk,qhc->khc', grad_scores, query_heads, preferred_element_ty...  3.69 us
    dot_general x1, matrix products, local(): lax.dot_general(block_rows, proj_rows, (((1,), (1,)), ((), ())), preferre...  3.5 us
  transfers between devices with their start and end apart: 5, of which 4 were waited for; matrix products, arithmetic and copies ran while one was open for 34% of the time, Pallas kernels for 0%

profile of v1, /device:TPU:0, one launch (start us, length us, event | category | flops | bytes accessed | tf_op | source)
XLA Modules:
  0.0 114.8 jit_solution(6037143701952601958)
XLA Ops:
  7.2 3.1 %collective-permute-start = (bf16[128,1024]{1,0:T(8,128)(2,1)}, bf16[128,1024]{1,0:T(8,128)(2,1)S(1)}, u32[]{:S(2)}, u32[]{:S(2)}) collective-permute-start(bf16[128,1024]{1,0:T(8,128)(2,1)} %bitcast.86), channel_id=1, source_target_pairs={{0,1},{1,2},{2,3},{3,0},{4,5},{5,6},{6,7},{7,4},{8,9},{9,10},{10,1... | collective-permute-start | bytes 786440 | tf_op jit(solution)/shard_map/ppermute | solution.py:51
  10.3 1.3 %copy.33 = bf16[1,512,640]{1,2,0:T(8,128)(2,1)S(1)} copy(bf16[1,512,640]{2,1,0:T(8,128)(2,1)} %param.10) | data formatting | bytes 1310720 | tf_op args[1]
  11.7 1.6 %copy.32 = bf16[1,512,640]{1,2,0:T(8,128)(2,1)S(1)} copy(bf16[1,512,640]{2,1,0:T(8,128)(2,1)} %param.9) | data formatting | bytes 1310720 | tf_op args[0]
  13.2 4.1 %fusion.28 = (f32[5,512]{1,0:T(8,128)S(1)}, f32[5,512,512]{1,2,0:T(8,128)}) fusion(bf16[512,5,128]{0,2,1:T(8,128)(2,1)S(1)} %bitcast.87, bf16[512,5,128]{0,2,1:T(8,128)(2,1)S(1)} %bitcast.80), kind=kOutput, calls=%fused_computation.50 | convolution fusion | flops 339476992 | bytes 6563840 | tf_op jit(solution)/shard_map/sub | solution.py:42
  17.4 1.5 %collective-permute-done = bf16[128,1024]{1,0:T(8,128)(2,1)S(1)} collective-permute-done((bf16[128,1024]{1,0:T(8,128)(2,1)}, bf16[128,1024]{1,0:T(8,128)(2,1)S(1)}, u32[]{:S(2)}, u32[]{:S(2)}) %collective-permute-start) | collective-permute-done | bytes 262176 | tf_op jit(solution)/shard_map/ppermute | solution.py:51
  19.0 3.2 %fusion.10 = bf16[5,512,512]{1,2,0:T(8,128)(2,1)S(1)} fusion(f32[5,512,512]{1,2,0:T(8,128)} %get-tuple-element.27, f32[5,512]{1,0:T(8,128)S(1)} %get-tuple-element.26), kind=kLoop, calls=%fused_computation.16 | loop fusion | flops 2621440 | bytes 7874560 | tf_op jit(solution)/shard_map/convert_element_type | solution.py:43
  22.3 1.3 %copy.37 = bf16[1,512,640]{1,2,0:T(8,128)(2,1)S(1)} copy(bf16[1,512,640]{2,1,0:T(8,128)(2,1)} %param.11) | data formatting | bytes 1310720 | tf_op args[2]
  23.6 4.6 %collective-permute-done.1 = bf16[128,1024]{1,0:T(8,128)(2,1)} collective-permute-done((bf16[128,1024]{1,0:T(8,128)(2,1)S(1)}, bf16[128,1024]{1,0:T(8,128)(2,1)}, u32[]{:S(2)}, u32[]{:S(2)}) %collective-permute-start.1) | collective-permute-done | bytes 262176 | tf_op jit(solution)/shard_map/ppermute | solution.py:51
  28.8 8.1 %collective-permute-done.2 = bf16[128,1024]{1,0:T(8,128)(2,1)S(1)} collective-permute-done((bf16[128,1024]{1,0:T(8,128)(2,1)}, bf16[128,1024]{1,0:T(8,128)(2,1)S(1)}, u32[]{:S(2)}, u32[]{:S(2)}) %collective-permute-start.2) | collective-permute-done | bytes 262176 | tf_op jit(solution)/shard_map/ppermute | solution.py:51
  39.0 4.5 %fusion.7 = (bf16[5,128,1024]{2,1,0:T(8,128)(2,1)}, bf16[1,5,128,1024]{3,2,1,0:T(8,128)(2,1)}, bf16[1,5,128,1024]{3,2,1,0:T(8,128)(2,1)}) fusion(bf16[1,5,128,1024]{3,2,1,0:T(8,128)(2,1)S(1)} %copy-done.10, bf16[1,5,128,1024]{3,2,1,0:T(8,128)(2,1)S(1)} %copy-done.11, bf16[1,5,128,1024]{3,2,1,0:T(8,128)(2,1)S(1)} %copy-done.12, ...), kind=kOutput, calls=%fused_computation.11 | convolution fusion | flops 686161920 | bytes 10878980 | tf_op jit(solution)/shard_map/dot_general | solution.py:61
  43.6 3.1 %convert_element_type.82 = f32[5,128,1024]{2,1,0:T(8,128)} convert(bf16[5,128,1024]{2,1,0:T(8,128)(2,1)} %param.16) | non-fusion elementwise | flops 655360 | bytes 3932160 | tf_op jit(solution)/shard_map/convert_element_type | solution.py:93
  46.7 31.9 %reduce-scatter.2.cloned.1.call-done = bf16[5,16,1024]{2,1,0:T(8,128)(2,1)} async-done(((bf16[5,128,1024]{2,1,0:T(8,128)(2,1)}), bf16[5,16,1024]{2,1,0:T(8,128)(2,1)}) %reduce-scatter.2.cloned.1.call-update) | async-done | bytes 163856 | tf_op jit(solution)/shard_map/reduce_scatter | solution.py:97
  78.6 1.9 %subtract_convert_fusion = (bf16[5,16,1024]{2,1,0:T(8,128)(2,1)}, f32[5,16,1024]{2,1,0:T(8,128)}) fusion(bf16[5,16,1024]{2,1,0:T(8,128)(2,1)} %reduce-scatter.2.cloned.1.call-done, f32[5,128,1024]{2,1,0:T(8,128)} %convert_element_type.82, s32[]{:T(128)S(6)} %select_n.18, f32[5,16,1024]{2,1,0:T(8,128)S(1)} %copy-done.8), kind=kLoop, calls=%fused_computation.36 | loop fusion | flops 737280 | bytes 1310724 | tf_op jit(solution)/shard_map/convert_element_type | solution.py:103
  80.6 3.5 %convolution_convert_fusion = bf16[512,640]{1,0:T(8,128)(2,1)} fusion(bf16[640,1024]{1,0:T(8,128)(2,1)} %bitcast.90, bf16[1024,1024]{1,0:T(8,128)(2,1)} %copy-done.9, s32[]{:T(128)S(6)} %select_n.17), kind=kOutput, calls=%fused_computation.22 | convolution fusion | flops 671416320 | bytes 3014660 | tf_op jit(solution)/shard_map/dot_general | solution.py:57
  84.1 1.3 %copy.36 = bf16[512,640]{0,1:T(8,128)(2,1)S(1)} copy(bf16[512,640]{1,0:T(8,128)(2,1)} %convolution_convert_fusion) | data formatting | bytes 1310720 | tf_op jit(solution)/shard_map/convert_element_type | solution.py:59
  86.7 3.8 %multiply_convert_fusion = bf16[5,512,512]{1,2,0:T(8,128)(2,1)S(1)} fusion(f32[5,512]{1,0:T(8,128)S(1)} %fusion.17, bf16[512,5,128]{0,2,1:T(8,128)(2,1)S(1)} %bitcast.78, bf16[512,5,128]{0,2,1:T(8,128)(2,1)} %bitcast.83, f32[5,512,512]{1,2,0:T(8,128)} %get-tuple-element.27, f32[5,512]{1,0:T(8,128)S(1)} %get-tuple-element.26), kind=kOutput, calls=%fused_computation.1 | convolution fusion | flops 340787200 | bytes 9195520 | tf_op jit(solution)/shard_map/qhc,khc->hqk/dot_general | solution.py:69
  90.5 1.5 %copy-done = bf16[5,512,512]{1,2,0:T(8,128)(2,1)} copy-done((bf16[5,512,512]{1,2,0:T(8,128)(2,1)}, bf16[5,512,512]{1,2,0:T(8,128)(2,1)S(1)}, u32[]{:S(2)}) %copy-start) | copy-done | bytes 2621464
  92.0 1.4 %fusion.13 = bf16[5,512,128]{1,2,0:T(8,128)(2,1)} fusion(bf16[512,5,128]{0,2,1:T(8,128)(2,1)S(1)} %bitcast.81, bf16[5,512,512]{1,2,0:T(8,128)(2,1)S(1)} %multiply_convert_fusion), kind=kOutput, calls=%fused_computation.21 | convolution fusion | flops 336199680 | bytes 3932160 | tf_op jit(solution)/shard_map/hqk,khc->qhc/dot_general | solution.py:75
  93.4 2.2 %copy.45 = bf16[1,512,640]{2,1,0:T(8,128)(2,1)} copy(bf16[1,512,640]{1,2,0:T(8,128)(2,1)} %bitcast.85) | data formatting | bytes 1310720
  95.6 3.7 %fusion.12 = bf16[5,512,128]{1,2,0:T(8,128)(2,1)} fusion(bf16[5,512,512]{1,2,0:T(8,128)(2,1)} %copy-done, bf16[512,5,128]{0,2,1:T(8,128)(2,1)} %bitcast.88), kind=kOutput, calls=%fused_computation.20 | convolution fusion | flops 336199680 | bytes 3932160 | tf_op jit(solution)/shard_map/hqk,qhc->khc/dot_general | solution.py:79
  99.3 2.2 %copy.46 = bf16[1,512,640]{2,1,0:T(8,128)(2,1)} copy(bf16[1,512,640]{1,2,0:T(8,128)(2,1)} %bitcast.89) | data formatting | bytes 1310720
  101.5 1.8 %convolution_convert_fusion.2 = bf16[5,128,512]{2,1,0:T(8,128)(2,1)} fusion(bf16[512,5,128]{0,2,1:T(8,128)(2,1)S(1)} %bitcast.79, bf16[5,512,512]{1,2,0:T(8,128)(2,1)S(1)} %fusion.10), kind=kOutput, calls=%fused_computation.24 | convolution fusion | flops 335872000 | bytes 3932160 | tf_op jit(solution)/shard_map/hqk,qhc->khc/dot_general | solution.py:66
  103.3 2.2 %copy.47 = bf16[1,512,640]{2,1,0:T(8,128)(2,1)} copy(bf16[1,512,640]{1,2,0:T(8,128)(2,1)} %bitcast.84) | data formatting | bytes 1310720
  105.4 2.5 %copy.74 = bf16[5,128,1024]{2,1,0:T(8,128)(2,1)} copy(bf16[5,128,1024]{2,1,0:T(8,128)(2,1)} %all-gather.2.cloned.1.call-done) | data formatting | bytes 2621440
  (42 shorter events, 4.2 us)
Async XLA Ops:
  7.2 71.5 %reduce-scatter.2.cloned.1.call-start = ((), (), s32[]{:S(2)}) async-start(), calls=%async_computation.1 | async-start | bytes 1474560 | tf_op jit(solution)/shard_map/reduce_scatter | solution.py:97
  7.2 11.6 %collective-permute-start = (bf16[128,1024]{1,0:T(8,128)(2,1)}, bf16[128,1024]{1,0:T(8,128)(2,1)S(1)}, u32[]{:S(2)}, u32[]{:S(2)}) collective-permute-start(bf16[128,1024]{1,0:T(8,128)(2,1)} %bitcast.86), channel_id=1, source_target_pairs={{0,1},{1,2},{2,3},{3,0},{4,5},{5,6},{6,7},{7,4},{8,9},{9,10},{10,1... | collective-permute-start | bytes 786440 | tf_op jit(solution)/shard_map/ppermute | solution.py:51
  11.7 5.7 %copy-start.1 = (bf16[1,512,640]{1,2,0:T(8,128)(2,1)}, bf16[1,512,640]{1,2,0:T(8,128)(2,1)S(1)}, u32[]{:S(2)}) copy-start(bf16[1,512,640]{1,2,0:T(8,128)(2,1)S(1)} %copy.33) | copy-start | bytes 1966084
  13.2 4.1 %copy-start.7 = (bf16[1,512,640]{1,2,0:T(8,128)(2,1)}, bf16[1,512,640]{1,2,0:T(8,128)(2,1)S(1)}, u32[]{:S(2)}) copy-start(bf16[1,512,640]{1,2,0:T(8,128)(2,1)S(1)} %copy.32) | copy-start | bytes 1966084
  18.9 9.4 %collective-permute-start.1 = (bf16[128,1024]{1,0:T(8,128)(2,1)S(1)}, bf16[128,1024]{1,0:T(8,128)(2,1)}, u32[]{:S(2)}, u32[]{:S(2)}) collective-permute-start(bf16[128,1024]{1,0:T(8,128)(2,1)S(1)} %collective-permute-done), channel_id=1, source_target_pairs={{0,1},{1,2},{2,3},{3,0},{4,5},{5,6},{6,7},{7,4},{8,9},{9,10},{10,1... | collective-permute-start | bytes 786440 | tf_op jit(solution)/shard_map/ppermute | solution.py:51
  23.6 14.3 %copy-start.3 = (bf16[1,512,640]{1,2,0:T(8,128)(2,1)}, bf16[1,512,640]{1,2,0:T(8,128)(2,1)S(1)}, u32[]{:S(2)}) copy-start(bf16[1,512,640]{1,2,0:T(8,128)(2,1)S(1)} %copy.37) | copy-start | bytes 1966084
  28.2 8.6 %collective-permute-start.2 = (bf16[128,1024]{1,0:T(8,128)(2,1)}, bf16[128,1024]{1,0:T(8,128)(2,1)S(1)}, u32[]{:S(2)}, u32[]{:S(2)}) collective-permute-start(bf16[128,1024]{1,0:T(8,128)(2,1)} %collective-permute-done.1), channel_id=1, source_target_pairs={{0,1},{1,2},{2,3},{3,0},{4,5},{5,6},{6,7},{7,4},{8,9},{9,10},{10,1... | collective-permute-start | bytes 786440 | tf_op jit(solution)/shard_map/ppermute | solution.py:51
  28.2 9.7 %copy-start.6 = (bf16[1,128,1024]{2,1,0:T(8,128)(2,1)S(1)}, bf16[1,128,1024]{2,1,0:T(8,128)(2,1)}, u32[]{:S(2)}) copy-start(bf16[1,128,1024]{2,1,0:T(8,128)(2,1)} %param.12) | copy-start | bytes 786436
  28.2 10.7 %copy-start.12 = (bf16[1,5,128,1024]{3,2,1,0:T(8,128)(2,1)S(1)}, bf16[1,5,128,1024]{3,2,1,0:T(8,128)(2,1)}, u32[]{:S(2)}) copy-start(bf16[1,5,128,1024]{3,2,1,0:T(8,128)(2,1)} %param.13) | copy-start | bytes 3932164
  28.8 14.7 %copy-start.4 = (bf16[5,512,128]{1,2,0:T(8,128)(2,1)}, bf16[5,512,128]{1,2,0:T(8,128)(2,1)S(1)}, u32[]{:S(2)}) copy-start(bf16[5,512,128]{1,2,0:T(8,128)(2,1)S(1)} %convolution_convert_fusion.1) | copy-start | bytes 1966084
  28.8 10.2 %copy-start.5 = (bf16[5,128,1024]{2,1,0:T(8,128)(2,1)S(1)}, bf16[5,128,1024]{2,1,0:T(8,128)(2,1)}, u32[]{:S(2)}) copy-start(bf16[5,128,1024]{2,1,0:T(8,128)(2,1)} %param.16) | copy-start | bytes 3932164
  28.8 10.2 %copy-start.10 = (bf16[1,5,128,1024]{3,2,1,0:T(8,128)(2,1)S(1)}, bf16[1,5,128,1024]{3,2,1,0:T(8,128)(2,1)}, u32[]{:S(2)}) copy-start(bf16[1,5,128,1024]{3,2,1,0:T(8,128)(2,1)} %param.14) | copy-start | bytes 3932164
  28.8 10.2 %copy-start.11 = (bf16[1,5,128,1024]{3,2,1,0:T(8,128)(2,1)S(1)}, bf16[1,5,128,1024]{3,2,1,0:T(8,128)(2,1)}, u32[]{:S(2)}) copy-start(bf16[1,5,128,1024]{3,2,1,0:T(8,128)(2,1)} %param.15) | copy-start | bytes 3932164
  39.0 4.5 %copy-start.9 = (bf16[1024,1024]{1,0:T(8,128)(2,1)}, bf16[1024,1024]{1,0:T(8,128)(2,1)S(1)}, u32[]{:S(2)}) copy-start(bf16[1024,1024]{1,0:T(8,128)(2,1)S(1)} %constant_dynamic-update-slice_fusion) | copy-start | bytes 6291460
  43.5 35.2 %copy-start.8 = (f32[5,16,1024]{2,1,0:T(8,128)S(1)}, f32[5,16,1024]{2,1,0:T(8,128)}, u32[]{:S(2)}) copy-start(f32[5,16,1024]{2,1,0:T(8,128)} %param.17) | copy-start | bytes 983044
  43.5 61.9 %all-gather.2.cloned.1.call-start = ((), (), s32[]{:S(2)}) async-start(), calls=%async_computation.2 | async-start | bytes 1474560 | tf_op jit(solution)/shard_map/all_gather | solution.py:106
  86.7 5.3 %copy-start.2 = (bf16[1,512,640]{1,2,0:T(8,128)(2,1)S(1)}, bf16[1,512,640]{1,2,0:T(8,128)(2,1)}, u32[]{:S(2)}) copy-start(bf16[1,512,640]{1,2,0:T(8,128)(2,1)} %copy-done.1) | copy-start | bytes 1966084
  90.5 1.5 %copy-start = (bf16[5,512,512]{1,2,0:T(8,128)(2,1)}, bf16[5,512,512]{1,2,0:T(8,128)(2,1)S(1)}, u32[]{:S(2)}) copy-start(bf16[5,512,512]{1,2,0:T(8,128)(2,1)S(1)} %multiply_convert_fusion) | copy-start | bytes 7864324
Sparse Core Ops, SparseCore 0:
  43.6 34.9 reduce-scatter.1
  80.7 24.4 all-gather.1
